TPU v7x, 32 devices: a whole 2x2x4 slice. The times are simulated.
32 devices in a mesh: wave: 8 (over z, y), lev: 4 (over x, core).
Axes of the slice: x: 2, y: 2, z: 4, core: 2. Of those that a mesh axis runs over, the one named last changes fastest.
Arguments:
- fine_state: float32 [8, 3, 2, 24, 49], P('lev', None, None, 'wave'), may hold values from -6 to 6
- fold_pairs: int32 [24], replicated, may hold values from 0 to 23, each once
- legendre: bfloat16 [24, 96, 49], P('wave', 'lev'), may hold values from -0.875 to 0.875
- gauss_weights: float32 [96], P('lev'), may hold values from 0.5 to 3
- grid_coef: float32 [8, 2560], replicated, may hold values from -4 to 4
- modes_from: float32 [8, 8], replicated
- modes_to: float32 [8, 8], replicated, as said below
- mode_rates: float32 [8], replicated, may hold values from 0.2 to 20
Outputs:
- corrected: float32 [8, 2, 2, 24, 49], P('lev', None, None, 'wave')
- fine_tend: float32 [8, 3, 2, 24, 49], P('lev', None, None, 'wave')
Inputs may be any that keep to these rules, and one draw needn't show every extreme that they name: Slot p holds zonal wavenumbers fold_pairs[p] and 47 - fold_pairs[p]; every value occurs once. modes_to is the inverse of modes_from.
All inputs are finite; a program needn't handle non-finite values.
Results may differ from a plain program's by a relative error of at most 0.02.
Values may be sent and summed in bfloat16 or wider, within the bound.
No kernel may reach another device: no remote copies, remote signals or barrier semaphores. Data moves between devices by JAX's collectives and lax.ppermute only.
A program may use at most 64 MiB of HBM per device.

v0:
```python
import math
import jax
import jax.numpy as jnp
from jax import lax
from jax.sharding import PartitionSpec as P

STEP_HALF = 0.5
quad_weights = ((5.0 / 24.0, 1.0 / 3.0, -1.0 / 24.0), (-1.0 / 24.0, 1.0 / 3.0, 5.0 / 24.0))
HIGHEST = lax.Precision.HIGHEST


def fourier_table(waves, points, amplitude):
    steps = jnp.arange(points, dtype=jnp.int32)
    turns = waves[:, :, None] * steps[None, None, :] % points
    angles = turns.astype(jnp.float32) * (2.0 * math.pi / points)
    return jnp.stack([jnp.cos(angles) * amplitude, -jnp.sin(angles) * amplitude]).astype(
        jnp.bfloat16
    )


def fine_rows(small_wave, fine_width):
    row_ids = jnp.arange(fine_width + 1, dtype=jnp.int32)[None, :]
    return row_ids < fine_width - small_wave[:, None]


def coarse_rows(small_wave, coarse):
    row_ids = jnp.arange(coarse, dtype=jnp.int32)[None, :]
    coarse_keep = row_ids < coarse - small_wave[:, None]
    degree = (small_wave[:, None] + row_ids).astype(jnp.float32)
    return (coarse_keep, degree)


def legendre_inverse(spectral, legendre_table, row_mask):
    split_spec = spectral[:, :, :, :, None, :] * row_mask[None, None, None]
    return jnp.einsum(
        "abcpmr,plr->abcpml", split_spec, legendre_table, preferred_element_type=jnp.float32
    ).astype(jnp.bfloat16)


def legendre_forward(returned, legendre_table, row_mask):
    members = jnp.einsum(
        "abcpml,plr->abcpmr", returned, legendre_table, preferred_element_type=jnp.float32
    )
    return jnp.sum(members * row_mask.astype(jnp.float32)[None, None, None], axis=4)


def grid_step(fourier, wave_table, coef, weights, factor):
    grid_field = jnp.einsum(
        "abcpmz,cpmk->abzk", fourier, wave_table, preferred_element_type=jnp.float32
    )
    product = (coef[:, None, None, :] * grid_field * grid_field).astype(jnp.bfloat16)
    returned = jnp.einsum(
        "abzk,cpmk->abcpmz", product, wave_table, preferred_element_type=jnp.float32
    )
    return (returned * (weights * factor)).astype(jnp.bfloat16)


def mix(matrix, values):
    return jnp.einsum("ql,lbcpr->qbcpr", matrix, values, precision=HIGHEST)


def per_device(
    fine_state, fold_pairs, legendre, gauss_weights, grid_coef, modes_from, modes_to, mode_rates
):
    n_wave = lax.axis_size("wave")
    wave_idx = lax.axis_index("wave")
    lev_idx = lax.axis_index("lev")
    lev_dev = fine_state.shape[0]
    pairs_dev = fine_state.shape[3]
    fine_width = fine_state.shape[4] - 1
    coarse = fine_width // 2
    longitudes = grid_coef.shape[1]
    band_size = legendre.shape[1] // n_wave
    small_wave = lax.dynamic_slice_in_dim(fold_pairs, wave_idx * pairs_dev, pairs_dev)
    first_member = fine_rows(small_wave, fine_width)
    member_mask = jnp.stack([first_member, jnp.logical_not(first_member)], 1).astype(jnp.bfloat16)
    coarse_keep, degree = coarse_rows(small_wave, coarse)
    keep_mask = coarse_keep[:, None, :].astype(jnp.bfloat16)
    keep_float = coarse_keep.astype(jnp.float32)
    fine_table = fourier_table(
        jnp.stack([fold_pairs, fine_width - 1 - fold_pairs], 1), longitudes, fine_width ** (-0.5)
    )
    coarse_table = fourier_table(fold_pairs[:, None], longitudes // 2, coarse ** (-0.5))
    coarse_leg = legendre[:, :, :coarse]
    coarse_coef = grid_coef[:, ::2]
    band_gauss = lax.dynamic_slice_in_dim(gauss_weights, wave_idx * band_size, band_size)
    local_to = lax.dynamic_slice_in_dim(modes_to, lev_idx * lev_dev, lev_dev, 1)
    local_from = lax.dynamic_slice_in_dim(modes_from, lev_idx * lev_dev, lev_dev, 1)
    mode_decay = lax.dynamic_slice_in_dim(mode_rates, lev_idx * lev_dev, lev_dev)

    def project(partial_sum):
        return mix(modes_to, partial_sum)

    def coarse_start(modes):
        gathered = lax.all_gather(modes, "lev", axis=0, tiled=True)
        levels = (mix(modes_from, gathered) * keep_float).astype(jnp.bfloat16)
        return legendre_inverse(levels, coarse_leg, keep_mask)

    def coarse_grid_step(fourier):
        return grid_step(
            fourier, coarse_table, coarse_coef, band_gauss, 2.0 * coarse / (longitudes // 2)
        )

    def coarse_finish(returned):
        partial_sum = legendre_forward(returned, coarse_leg, keep_mask)
        return lax.psum_scatter(
            project(partial_sum).astype(jnp.bfloat16), "lev", scatter_dimension=0, tiled=True
        ).astype(jnp.float32)

    def coarse_eval(modes):
        fourier = lax.all_to_all(
            coarse_start(modes), "wave", split_axis=5, concat_axis=3, tiled=True
        )
        returned = lax.all_to_all(
            coarse_grid_step(fourier), "wave", split_axis=3, concat_axis=5, tiled=True
        )
        return coarse_finish(returned)

    restricted = fine_state[..., :coarse] * keep_float
    fine_spec = lax.all_gather(fine_state.astype(jnp.bfloat16), "lev", axis=0, tiled=True)
    fine_fourier = legendre_inverse(fine_spec, legendre, member_mask)
    fine_fourier = lax.all_to_all(fine_fourier, "wave", split_axis=5, concat_axis=3, tiled=True)
    fine_back = lax.all_to_all(
        grid_step(fine_fourier, fine_table, grid_coef, band_gauss, 2.0 * fine_width / longitudes),
        "wave",
        split_axis=3,
        concat_axis=5,
        tiled=True,
    )
    fine_tend = lax.psum_scatter(
        legendre_forward(fine_back, legendre, member_mask).astype(jnp.bfloat16),
        "lev",
        scatter_dimension=0,
        tiled=True,
    ).astype(jnp.float32)
    restricted_tend = fine_tend[..., :coarse] * keep_float
    stacked = jnp.concatenate([restricted, restricted_tend], 1)
    both_modes = lax.psum_scatter(
        mix(local_to, stacked).astype(jnp.bfloat16), "lev", scatter_dimension=0, tiled=True
    ).astype(jnp.float32)
    nodes = fine_state.shape[1]
    old_state = both_modes[:, :nodes]
    old_tend = both_modes[:, nodes:]
    old_coarse = coarse_eval(old_state[:, 1:2])
    stiffness = (
        mode_decay[:, None, None, None]
        * (degree * (degree + 1.0) / (coarse * (coarse + 1.0)))[None, None]
    )
    source = old_tend - stiffness[:, None] * old_state
    integral_mid = (
        quad_weights[0][0] * source[:, 0]
        + quad_weights[0][1] * source[:, 1]
        + quad_weights[0][2] * source[:, 2]
    )
    integral_end = (
        quad_weights[1][0] * source[:, 0]
        + quad_weights[1][1] * source[:, 1]
        + quad_weights[1][2] * source[:, 2]
    )
    divisor = 1.0 + STEP_HALF * stiffness
    next_mid = (old_state[:, 0] + STEP_HALF * stiffness * old_state[:, 1] + integral_mid) / divisor
    coarse_fresh = coarse_eval(next_mid[:, None])
    next_end = (
        next_mid
        + STEP_HALF * (coarse_fresh[:, 0] - old_coarse[:, 0])
        + STEP_HALF * stiffness * old_state[:, 2]
        + integral_end
    ) / divisor
    change = jnp.stack([next_mid - old_state[:, 1], next_end - old_state[:, 2]], 1)
    lifted = lax.psum_scatter(
        mix(local_from, change).astype(jnp.bfloat16), "lev", scatter_dimension=0, tiled=True
    ).astype(jnp.float32)
    corrected = fine_state[:, 1:] + jnp.pad(
        lifted, ((0, 0), (0, 0), (0, 0), (0, 0), (0, fine_width + 1 - coarse))
    )
    return (corrected, fine_tend)


def solution(mesh):
    placed = (
        P("lev", None, None, "wave", None),
        P(),
        P("wave", "lev", None),
        P("lev"),
        P(),
        P(),
        P(),
        P(),
    )
    return jax.shard_map(
        per_device,
        mesh=mesh,
        in_specs=placed,
        out_specs=(P("lev", None, None, "wave", None), P("lev", None, None, "wave", None)),
        check_vma=False,
    )
```

profile of v0, /device:TPU:0, one launch (start us, length us, event | category | flops | bytes accessed | tf_op | source)
XLA Modules:
  0.0 130.4 jit_solution(1549815140402897033)
XLA Ops:
  0.6 0.0 copy-start
  0.7 0.7 broadcast_subtract_fusion.1
  1.4 0.1 iota_compare_fusion.1
  1.5 6.2 %all_gather.9 = bf16[8,3,2,3,49]{4,2,3,1,0:T(2,128)(2,1)S(1)} all-gather(bf16[2,3,2,3,49]{4,2,3,1,0:T(2,128)(2,1)S(1)} %convert_element_type.212), channel_id=1, replica_groups=mesh['wave'=8,'lev'=4] {'lev'}, dimensions={0}, use_global_device_ids=true | all-gather | bytes 17640 | tf_op jit(solution)/shard_map/all_gather | solution.py:120
  7.7 0.7 copy-done.1
  8.4 0.1 fusion.2
  8.6 0.2 copy.95
  8.7 0.8 reshape.468
  9.6 6.4 %all-to-all-start = ((bf16[8,2,432]{2,1,0:T(2,128)(2,1)}), bf16[8,2,432]{2,1,0:T(2,128)(2,1)S(1)}, u32[]{:S(2)}, u32[]{:S(2)}) async-start(bf16[8,2,432]{2,1,0:T(2,128)(2,1)} %reshape.468), calls=%async_computation | async-start | bytes 32768 | tf_op jit(solution)/shard_map/all_to_all | solution.py:122
  16.0 0.1 fusion.97
  16.1 0.6 multiply_convert_fusion.3
  16.7 2.3 %multiply_convert_fusion.1 = (bf16[1,24,2,2560]{3,1,2,0:T(8,128)(2,1)S(1)}, bf16[1,24,2,2560]{3,1,2,0:T(8,128)(2,1)S(1)}) fusion(s32[24,2]{0,1:T(2,128)S(1)} %pad_add_fusion), kind=kLoop, calls=%fused_computation.52 | loop fusion | flops 1720320 | bytes 491712 | tf_op jit(solution)/shard_map/convert.4
  19.1 0.6 copy-done.6
  19.7 0.1 dynamic_slice.19
  19.8 0.1 broadcast_multiply_fusion
  19.9 0.6 copy-done.7
  20.4 0.1 dynamic-slice_multiply_fusion
  20.5 2.1 %all-to-all-done = bf16[8,2,432]{2,1,0:T(2,128)(2,1)S(1)} async-done(((bf16[8,2,432]{2,1,0:T(2,128)(2,1)}), bf16[8,2,432]{2,1,0:T(2,128)(2,1)S(1)}, u32[]{:S(2)}, u32[]{:S(2)}) %all-to-all-start) | async-done | bytes 13856 | tf_op jit(solution)/shard_map/all_to_all | solution.py:122
  22.6 0.2 reshape.469
  22.8 0.2 copy.97
  23.0 0.7 copy-done.3
  23.7 0.8 fusion.3
  24.6 0.2 copy.99
  24.7 0.8 reshape.470
  25.6 3.9 %all-to-all-start.1 = ((bf16[8,2,432]{2,1,0:T(2,128)(2,1)}), bf16[8,2,432]{2,1,0:T(2,128)(2,1)S(1)}, u32[]{:S(2)}, u32[]{:S(2)}) async-start(bf16[8,2,432]{2,1,0:T(2,128)(2,1)} %reshape.470), calls=%async_computation.1 | async-start | bytes 32768 | tf_op jit(solution)/shard_map/all_to_all | solution.py:123
  29.5 0.1 fusion.110
  29.5 1.4 %slice.58 = f32[8,1280]{1,0:T(8,128)S(1)} slice(f32[8,2560]{1,0:T(8,128)S(1)} %copy-done.3), slice={[0:8:1], [0:2560:2]} | slice | bytes 81920 | tf_op jit(solution)/shard_map/slice | solution.py:85
  31.0 0.6 copy-done.8
  31.6 0.6 dynamic-slice
  32.9 3.2 %all-to-all-done.1 = bf16[8,2,432]{2,1,0:T(2,128)(2,1)S(1)} async-done(((bf16[8,2,432]{2,1,0:T(2,128)(2,1)}), bf16[8,2,432]{2,1,0:T(2,128)(2,1)S(1)}, u32[]{:S(2)}, u32[]{:S(2)}) %all-to-all-start.1) | async-done | bytes 13856 | tf_op jit(solution)/shard_map/all_to_all | solution.py:123
  36.0 0.2 reshape.471
  36.3 0.2 copy.101
  36.4 0.2 fusion
  36.7 10.5 %all-reduce.1 = bf16[8,3,2,3,49]{4,0,3,2,1:T(8,128)(2,1)S(1)} all-reduce(bf16[8,3,2,3,49]{4,0,3,2,1:T(8,128)(2,1)S(1)} %copy.103), channel_id=2, replica_groups=mesh['wave'=8,'lev'=4] {'lev'}, use_global_device_ids=true, to_apply=%region_1.2.clone | all-reduce | flops 7056 | bytes 28224
  47.2 0.3 convolution_convert_fusion
  47.6 11.7 %all-reduce.2 = bf16[8,6,2,3,24]{4,0,3,2,1:T(8,128)(2,1)S(1)} all-reduce(bf16[8,6,2,3,24]{4,0,3,2,1:T(8,128)(2,1)S(1)} %convolution_convert_fusion), channel_id=3, replica_groups=mesh['wave'=8,'lev'=4] {'lev'}, use_global_device_ids=true, to_apply=%region_2.3.clone | all-reduce | flops 6912 | bytes 27648
  59.4 5.2 %all_gather.10 = f32[8,1,2,3,24]{4,2,3,1,0:T(2,128)S(1)} all-gather(f32[2,1,2,3,24]{4,2,3,1,0:T(2,128)S(1)} %copy.104), channel_id=1, replica_groups=mesh['wave'=8,'lev'=4] {'lev'}, dimensions={0}, use_global_device_ids=true | all-gather | bytes 5760 | tf_op jit(solution)/shard_map/all_gather | solution.py:95
  64.6 0.2 fusion.23
  64.8 0.1 fusion.14
  64.9 0.7 copy.106
  65.6 3.3 %all-to-all-start.2 = ((bf16[8,1,2,3,1,24]{0,2,3,4,1,5:T(2,128)(2,1)}), bf16[8,1,2,3,1,24]{0,2,3,4,1,5:T(2,128)(2,1)S(1)}, u32[]{:S(2)}, u32[]{:S(2)}) async-start(bf16[8,1,2,3,1,24]{0,2,3,4,1,5:T(2,128)(2,1)} %copy.106), calls=%async_computation.2 | async-start | bytes 73728 | tf_op jit(solution)/shard_map/all_to_all | solution.py:111
  69.0 5.2 %all_gather.11 = f32[8,1,2,3,24]{4,2,3,1,0:T(2,128)S(1)} all-gather(f32[2,1,2,3,24]{4,2,3,1,0:T(2,128)S(1)} %copy.114), channel_id=1, replica_groups=mesh['wave'=8,'lev'=4] {'lev'}, dimensions={0}, use_global_device_ids=true | all-gather | bytes 5760 | tf_op jit(solution)/shard_map/all_gather | solution.py:95
  74.2 0.2 fusion.20
  74.4 0.1 fusion.16
  74.5 0.6 copy.125
  75.1 0.7 copy.116
  75.8 5.9 %all-to-all-start.4 = ((bf16[8,1,2,3,1,24]{0,2,3,4,1,5:T(2,128)(2,1)}), bf16[8,1,2,3,1,24]{0,2,3,4,1,5:T(2,128)(2,1)S(1)}, u32[]{:S(2)}, u32[]{:S(2)}) async-start(bf16[8,1,2,3,1,24]{0,2,3,4,1,5:T(2,128)(2,1)} %copy.116), calls=%async_computation.4 | async-start | bytes 73728 | tf_op jit(solution)/shard_map/all_to_all | solution.py:111
  81.8 0.4 fusion.21
  82.2 0.8 copy.110
  82.9 5.5 %all-to-all-done.4 = bf16[8,1,2,3,1,24]{0,2,3,4,1,5:T(2,128)(2,1)S(1)} async-done(((bf16[8,1,2,3,1,24]{0,2,3,4,1,5:T(2,128)(2,1)}), bf16[8,1,2,3,1,24]{0,2,3,4,1,5:T(2,128)(2,1)S(1)}, u32[]{:S(2)}, u32[]{:S(2)}) %all-to-all-start.4) | async-done | bytes 2336 | tf_op jit(solution)/shard_map/all_to_all | solution.py:111
  88.4 3.3 %all-to-all-start.3 = ((bf16[8,1,2,24,1,3]{0,2,5,4,1,3:T(2,128)(2,1)}), bf16[8,1,2,24,1,3]{0,2,5,4,1,3:T(2,128)(2,1)S(1)}, u32[]{:S(2)}, u32[]{:S(2)}) async-start(bf16[8,1,2,24,1,3]{0,2,5,4,1,3:T(2,128)(2,1)} %copy.110), calls=%async_computation.3 | async-start | bytes 73728 | tf_op jit(solution)/shard_map/all_to_all | solution.py:114
  91.9 0.4 fusion.18
  92.2 0.7 copy.120
  93.0 5.5 %all-to-all-done.3 = bf16[8,1,2,24,1,3]{0,2,5,4,1,3:T(2,128)(2,1)S(1)} async-done(((bf16[8,1,2,24,1,3]{0,2,5,4,1,3:T(2,128)(2,1)}), bf16[8,1,2,24,1,3]{0,2,5,4,1,3:T(2,128)(2,1)S(1)}, u32[]{:S(2)}, u32[]{:S(2)}) %all-to-all-start.3) | async-done | bytes 2336 | tf_op jit(solution)/shard_map/all_to_all | solution.py:114
  98.4 3.3 %all-to-all-start.5 = ((bf16[8,1,2,24,1,3]{0,2,5,4,1,3:T(2,128)(2,1)}), bf16[8,1,2,24,1,3]{0,2,5,4,1,3:T(2,128)(2,1)S(1)}, u32[]{:S(2)}, u32[]{:S(2)}) async-start(bf16[8,1,2,24,1,3]{0,2,5,4,1,3:T(2,128)(2,1)} %copy.120), calls=%async_computation.5 | async-start | bytes 73728 | tf_op jit(solution)/shard_map/all_to_all | solution.py:114
  101.8 0.2 fusion.7
  102.0 0.2 fusion.15
  102.2 6.2 %all-to-all-done.5 = bf16[8,1,2,24,1,3]{0,2,5,4,1,3:T(2,128)(2,1)S(1)} async-done(((bf16[8,1,2,24,1,3]{0,2,5,4,1,3:T(2,128)(2,1)}), bf16[8,1,2,24,1,3]{0,2,5,4,1,3:T(2,128)(2,1)S(1)}, u32[]{:S(2)}, u32[]{:S(2)}) %all-to-all-start.5) | async-done | bytes 2336 | tf_op jit(solution)/shard_map/all_to_all | solution.py:114
  108.5 0.2 fusion.9
  108.7 0.2 fusion.17
  108.8 10.3 %all-reduce.6 = (bf16[8,1,2,3,24]{4,0,3,2,1:T(8,128)(2,1)S(1)}, bf16[8,1,2,3,24]{4,0,3,2,1:T(8,128)(2,1)S(1)}) all-reduce(bf16[8,1,2,3,24]{4,0,3,2,1:T(8,128)(2,1)S(1)} %fusion.17, bf16[8,1,2,3,24]{4,0,3,2,1:T(8,128)(2,1)S(1)} %fusion.15), channel_id=5, replica_groups=mesh['wave'=8,'lev'=4] {'lev'}, use_global_device_ids=true, to_apply=%region_4.5.clone | all-reduce | flops 2304 | bytes 9216
  119.1 0.2 convolution_convert_fusion.2
  119.4 10.4 %all-reduce.5 = bf16[8,2,2,3,24]{4,0,3,2,1:T(8,128)(2,1)S(1)} all-reduce(bf16[8,2,2,3,24]{4,0,3,2,1:T(8,128)(2,1)S(1)} %convolution_convert_fusion.2), channel_id=6, replica_groups=mesh['wave'=8,'lev'=4] {'lev'}, use_global_device_ids=true, to_apply=%region_5.6.clone | all-reduce | flops 2304 | bytes 9216
  129.8 0.6 copy.124
  (37 shorter events, 0.4 us)
Async XLA Ops:
  0.6 46.6 %copy-start = (f32[8,8]{1,0:T(8,128)S(1)}, f32[8,8]{1,0:T(8,128)}, u32[]{:S(2)}) copy-start(f32[8,8]{1,0:T(8,128)} %param.14) | copy-start | bytes 772
  0.6 0.8 copy-start.2
  7.7 0.7 copy-start.1
  9.6 6.4 %copy-start.5 = (s32[24]{0:T(128)S(1)}, s32[24]{0:T(128)}, u32[]{:S(2)}) copy-start(s32[24]{0:T(128)} %param.9) | copy-start | bytes 292
  9.6 13.0 %all-to-all-start = ((bf16[8,2,432]{2,1,0:T(2,128)(2,1)}), bf16[8,2,432]{2,1,0:T(2,128)(2,1)S(1)}, u32[]{:S(2)}, u32[]{:S(2)}) async-start(bf16[8,2,432]{2,1,0:T(2,128)(2,1)} %reshape.468), calls=%async_computation | async-start | bytes 32768 | tf_op jit(solution)/shard_map/all_to_all | solution.py:122
  19.0 0.7 copy-start.6
  19.8 0.7 copy-start.7
  22.8 0.9 copy-start.3
  25.6 10.5 %all-to-all-start.1 = ((bf16[8,2,432]{2,1,0:T(2,128)(2,1)}), bf16[8,2,432]{2,1,0:T(2,128)(2,1)S(1)}, u32[]{:S(2)}, u32[]{:S(2)}) async-start(bf16[8,2,432]{2,1,0:T(2,128)(2,1)} %reshape.470), calls=%async_computation.1 | async-start | bytes 32768 | tf_op jit(solution)/shard_map/all_to_all | solution.py:123
  31.0 0.7 copy-start.8
  59.3 5.3 %copy-start.4 = (f32[8,8]{1,0:T(8,128)S(1)}, f32[8,8]{1,0:T(8,128)}, u32[]{:S(2)}) copy-start(f32[8,8]{1,0:T(8,128)} %param.13) | copy-start | bytes 772
  65.6 10.2 %all-to-all-start.2 = ((bf16[8,1,2,3,1,24]{0,2,3,4,1,5:T(2,128)(2,1)}), bf16[8,1,2,3,1,24]{0,2,3,4,1,5:T(2,128)(2,1)S(1)}, u32[]{:S(2)}, u32[]{:S(2)}) async-start(bf16[8,1,2,3,1,24]{0,2,3,4,1,5:T(2,128)(2,1)} %copy.106), calls=%async_computation.2 | async-start | bytes 73728 | tf_op jit(solution)/shard_map/all_to_all | solution.py:111
  75.8 12.6 %all-to-all-start.4 = ((bf16[8,1,2,3,1,24]{0,2,3,4,1,5:T(2,128)(2,1)}), bf16[8,1,2,3,1,24]{0,2,3,4,1,5:T(2,128)(2,1)S(1)}, u32[]{:S(2)}, u32[]{:S(2)}) async-start(bf16[8,1,2,3,1,24]{0,2,3,4,1,5:T(2,128)(2,1)} %copy.116), calls=%async_computation.4 | async-start | bytes 73728 | tf_op jit(solution)/shard_map/all_to_all | solution.py:111
  88.4 10.0 %all-to-all-start.3 = ((bf16[8,1,2,24,1,3]{0,2,5,4,1,3:T(2,128)(2,1)}), bf16[8,1,2,24,1,3]{0,2,5,4,1,3:T(2,128)(2,1)S(1)}, u32[]{:S(2)}, u32[]{:S(2)}) async-start(bf16[8,1,2,24,1,3]{0,2,5,4,1,3:T(2,128)(2,1)} %copy.110), calls=%async_computation.3 | async-start | bytes 73728 | tf_op jit(solution)/shard_map/all_to_all | solution.py:114
  98.4 10.0 %all-to-all-start.5 = ((bf16[8,1,2,24,1,3]{0,2,5,4,1,3:T(2,128)(2,1)}), bf16[8,1,2,24,1,3]{0,2,5,4,1,3:T(2,128)(2,1)S(1)}, u32[]{:S(2)}, u32[]{:S(2)}) async-start(bf16[8,1,2,24,1,3]{0,2,5,4,1,3:T(2,128)(2,1)} %copy.120), calls=%async_computation.5 | async-start | bytes 73728 | tf_op jit(solution)/shard_map/all_to_all | solution.py:114
where the time goes:
time: 131 us; the launch traced here: 130 us
  blocking collectives  59.5 us (45%)
  starting transfers between devices  26.3 us (20%)
  waiting for transfers between devices  22.5 us (17%)
  local copies, waits for them, and re-layouts  12.5 us (10%)
  other arithmetic  4.17 us (3%)
  matrix products  3.8 us (3%)
  between operations  1.69 us (1%)
    unnamed x4, blocking collectives  42.8 us
    all_to_all x2, waiting for transfers between devices, coarse_eval(): lax.all_to_all(coarse_grid_step(fourier), 'wave', split_axis=3, concat_ax...  11.7 us
    all_gather x2, blocking collectives, coarse_start(): gathered = lax.all_gather(modes, 'lev', axis=0, tiled=True)  10.4 us
    all_to_all x2, starting transfers between devices, coarse_eval(): lax.all_to_all(coarse_start(modes), 'wave', split_axis=5, concat_axis=3,...  9.25 us
    unnamed x26, local copies, waits for them, and re-layouts  7.27 us
    all_to_all x2, starting transfers between devices, coarse_eval(): lax.all_to_all(coarse_grid_step(fourier), 'wave', split_axis=3, concat_ax...  6.68 us
    all_to_all x1, starting transfers between devices, per_device(): lax.all_to_all(fine_fourier, 'wave', split_axis=5, concat_axis=3, tiled=T...  6.43 us
    all_gather x1, blocking collectives, per_device(): lax.all_gather(fine_state.astype(jnp.bfloat16), 'lev', axis=0, tiled=True)  6.21 us
  transfers between devices with their start and end apart: 6, of which 5 were waited for; matrix products, arithmetic and copies ran while one was open for 7% of the time, Pallas kernels for 0%

commit v1 on v0

--- a/solution.py
+++ b/solution.py
@@ -92,7 +92,14 @@
         return mix(modes_to, partial_sum)
 
     def coarse_start(modes):
-        gathered = lax.all_gather(modes, "lev", axis=0, tiled=True)
+        ring = [modes]
+        for hop in range(3):
+            ring.append(lax.ppermute(ring[-1], "lev", [(dev, (dev + 1) % 4) for dev in range(4)]))
+        gathered = jnp.roll(
+            jnp.concatenate(ring[::-1], axis=0),
+            (lax.axis_index("lev") + 1) * ring[0].shape[0],
+            axis=0,
+        )
         levels = (mix(modes_from, gathered) * keep_float).astype(jnp.bfloat16)
         return legendre_inverse(levels, coarse_leg, keep_mask)
 

time: 131 us -> 132 us (level)
  waiting for transfers between devices: 22.5 us -> 33.2 us
  blocking collectives: 59.5 us -> 49.1 us
    all_gather x2 -> x0, blocking collectives: 10.4 us -> none  [coarse_start(): gathered = lax.all_gather(modes, 'lev', axis=0, tiled=True)]
    all_to_all x2, waiting for transfers between devices: 5.53 us -> 11 us  [coarse_eval(): lax.all_to_all(coarse_start(modes), 'wave', split_axis=5, concat_axis=3,...]
    ppermute x0 -> x6, starting transfers between devices: none -> 3.48 us  [coarse_start(): lax.ppermute(ring[-1], 'lev', [(dev, (dev + 1) % 4) for dev in range(4)])]
    ppermute x0 -> x6, waiting for transfers between devices: none -> 3.22 us  [coarse_start(): lax.ppermute(ring[-1], 'lev', [(dev, (dev + 1) % 4) for dev in range(4)])]
    all_to_all x2, starting transfers between devices: 9.25 us -> 6.68 us  [coarse_eval(): lax.all_to_all(coarse_start(modes), 'wave', split_axis=5, concat_axis=3,...]
    all_to_all x1, waiting for transfers between devices: 3.18 us -> 4.57 us  [per_device(): lax.all_to_all(grid_step(fine_fourier, fine_table, grid_coef, band_gauss,...]
  transfers between devices with their start and end apart: 6 -> 12, of which waited for: 5 -> 8; matrix products, arithmetic and copies ran while one was open for 7% -> 8% of each run, Pallas kernels for 0% -> 0%
where the time goes in v1:
time: 132 us; the launch traced here: 131 us
  blocking collectives  49.1 us (37%)
  waiting for transfers between devices  33.2 us (25%)
  starting transfers between devices  26.6 us (20%)
  local copies, waits for them, and re-layouts  12.5 us (9%)
  other arithmetic  4.17 us (3%)
  matrix products  3.97 us (3%)
  between operations  1.71 us (1%)
    unnamed x4, blocking collectives  42.8 us
    all_to_all x2, waiting for transfers between devices, coarse_eval(): lax.all_to_all(coarse_grid_step(fourier), 'wave', split_axis=3, concat_ax...  11.7 us
    all_to_all x2, waiting for transfers between devices, coarse_eval(): lax.all_to_all(coarse_start(modes), 'wave', split_axis=5, concat_axis=3,...  11 us
    unnamed x26, local copies, waits for them, and re-layouts  7.27 us
    all_to_all x2, starting transfers between devices, coarse_eval(): lax.all_to_all(coarse_grid_step(fourier), 'wave', split_axis=3, concat_ax...  6.68 us
    all_to_all x2, starting transfers between devices, coarse_eval(): lax.all_to_all(coarse_start(modes), 'wave', split_axis=5, concat_axis=3,...  6.68 us
    all_to_all x1, starting transfers between devices, per_device(): lax.all_to_all(fine_fourier, 'wave', split_axis=5, concat_axis=3, tiled=T...  6.43 us
    all_gather x1, blocking collectives, per_device(): lax.all_gather(fine_state.astype(jnp.bfloat16), 'lev', axis=0, tiled=True)  6.21 us
  transfers between devices with their start and end apart: 12, of which 8 were waited for; matrix products, arithmetic and copies ran while one was open for 8% of the time, Pallas kernels for 0%

profile of v1, /device:TPU:0, one launch (start us, length us, event | category | flops | bytes accessed | tf_op | source)
XLA Modules:
  0.0 131.2 jit_solution(15487430890582110499)
XLA Ops:
  0.7 0.7 broadcast_subtract_fusion.1
  1.4 0.1 iota_compare_fusion.1
  1.5 6.2 %all_gather.3 = bf16[8,3,2,3,49]{4,2,3,1,0:T(2,128)(2,1)S(1)} all-gather(bf16[2,3,2,3,49]{4,2,3,1,0:T(2,128)(2,1)S(1)} %convert_element_type.212), channel_id=1, replica_groups=mesh['wave'=8,'lev'=4] {'lev'}, dimensions={0}, use_global_device_ids=true | all-gather | bytes 17640 | tf_op jit(solution)/shard_map/all_gather | solution.py:127
  7.7 0.7 copy-done.1
  8.4 0.1 fusion.2
  8.6 0.2 copy.93
  8.7 0.8 reshape.468
  9.6 6.4 %all-to-all-start = ((bf16[8,2,432]{2,1,0:T(2,128)(2,1)}), bf16[8,2,432]{2,1,0:T(2,128)(2,1)S(1)}, u32[]{:S(2)}, u32[]{:S(2)}) async-start(bf16[8,2,432]{2,1,0:T(2,128)(2,1)} %reshape.468), calls=%async_computation | async-start | bytes 32768 | tf_op jit(solution)/shard_map/all_to_all | solution.py:129
  16.0 0.1 fusion.111
  16.1 2.3 %multiply_convert_fusion.1 = (bf16[1,24,2,2560]{3,1,2,0:T(8,128)(2,1)S(1)}, bf16[1,24,2,2560]{3,1,2,0:T(8,128)(2,1)S(1)}) fusion(s32[24,2]{0,1:T(2,128)S(1)} %pad_add_fusion), kind=kLoop, calls=%fused_computation.52 | loop fusion | flops 1720320 | bytes 491712 | tf_op jit(solution)/shard_map/convert.4
  18.5 0.6 copy-done.6
  19.3 0.6 copy-done.7
  19.8 0.1 dynamic-slice_multiply_fusion
  19.9 2.7 %all-to-all-done = bf16[8,2,432]{2,1,0:T(2,128)(2,1)S(1)} async-done(((bf16[8,2,432]{2,1,0:T(2,128)(2,1)}), bf16[8,2,432]{2,1,0:T(2,128)(2,1)S(1)}, u32[]{:S(2)}, u32[]{:S(2)}) %all-to-all-start) | async-done | bytes 13856 | tf_op jit(solution)/shard_map/all_to_all | solution.py:129
  22.6 0.2 reshape.469
  22.8 0.2 copy.95
  23.0 0.7 copy-done.3
  23.7 0.8 fusion.3
  24.6 0.2 copy.97
  24.7 0.8 reshape.470
  25.6 3.3 %all-to-all-start.1 = ((bf16[8,2,432]{2,1,0:T(2,128)(2,1)}), bf16[8,2,432]{2,1,0:T(2,128)(2,1)S(1)}, u32[]{:S(2)}, u32[]{:S(2)}) async-start(bf16[8,2,432]{2,1,0:T(2,128)(2,1)} %reshape.470), calls=%async_computation.1 | async-start | bytes 32768 | tf_op jit(solution)/shard_map/all_to_all | solution.py:130
  29.0 0.7 copy-done.8
  29.6 0.6 dynamic-slice
  30.9 4.6 %all-to-all-done.1 = bf16[8,2,432]{2,1,0:T(2,128)(2,1)S(1)} async-done(((bf16[8,2,432]{2,1,0:T(2,128)(2,1)}), bf16[8,2,432]{2,1,0:T(2,128)(2,1)S(1)}, u32[]{:S(2)}, u32[]{:S(2)}) %all-to-all-start.1) | async-done | bytes 13856 | tf_op jit(solution)/shard_map/all_to_all | solution.py:130
  35.5 0.2 reshape.471
  35.7 0.2 copy.99
  35.8 0.2 fusion
  36.1 10.5 %all-reduce.1 = bf16[8,3,2,3,49]{4,0,3,2,1:T(8,128)(2,1)S(1)} all-reduce(bf16[8,3,2,3,49]{4,0,3,2,1:T(8,128)(2,1)S(1)} %copy.101), channel_id=2, replica_groups=mesh['wave'=8,'lev'=4] {'lev'}, use_global_device_ids=true, to_apply=%region_1.2.clone | all-reduce | flops 7056 | bytes 28224
  46.6 0.3 convolution_convert_fusion
  47.0 11.7 %all-reduce.2 = bf16[8,6,2,3,24]{4,0,3,2,1:T(8,128)(2,1)S(1)} all-reduce(bf16[8,6,2,3,24]{4,0,3,2,1:T(8,128)(2,1)S(1)} %convolution_convert_fusion), channel_id=3, replica_groups=mesh['wave'=8,'lev'=4] {'lev'}, use_global_device_ids=true, to_apply=%region_2.3.clone | all-reduce | flops 6912 | bytes 27648
  58.8 1.1 collective-permute-start.3
  59.9 1.9 %collective-permute-done = f32[2,1,2,3,24]{4,0,3,2,1:T(2,128)S(1)} collective-permute-done((f32[2,1,2,3,24]{4,0,3,2,1:T(2,128)S(1)}, f32[2,1,2,3,24]{4,0,3,2,1:T(2,128)S(1)}, u32[]{:S(2)}, u32[]{:S(2)}) %collective-permute-start) | collective-permute-done | bytes 1184 | tf_op jit(solution)/shard_map/ppermute | solution.py:97
  61.9 0.6 multiply_convert_fusion.3
  62.5 1.2 collective-permute-start.4
  63.6 1.3 collective-permute-done.1
  64.9 1.4 %slice.58 = f32[8,1280]{1,0:T(8,128)S(1)} slice(f32[8,2560]{1,0:T(8,128)S(1)} %copy-done.3), slice={[0:8:1], [0:2560:2]} | slice | bytes 81920 | tf_op jit(solution)/shard_map/slice | solution.py:85
  66.4 0.6 copy.121
  67.0 1.1 collective-permute-start.5
  68.1 0.2 fusion.23
  68.4 0.1 fusion.14
  68.5 0.7 copy.103
  69.2 3.3 %all-to-all-start.2 = ((bf16[8,1,2,3,1,24]{0,2,3,4,1,5:T(2,128)(2,1)}), bf16[8,1,2,3,1,24]{0,2,3,4,1,5:T(2,128)(2,1)S(1)}, u32[]{:S(2)}, u32[]{:S(2)}) async-start(bf16[8,1,2,3,1,24]{0,2,3,4,1,5:T(2,128)(2,1)} %copy.103), calls=%async_computation.2 | async-start | bytes 73728 | tf_op jit(solution)/shard_map/all_to_all | solution.py:118
  72.6 0.3 fusion.20
  72.8 0.1 fusion.16
  73.0 0.7 copy.112
  73.7 5.5 %all-to-all-done.2 = bf16[8,1,2,3,1,24]{0,2,3,4,1,5:T(2,128)(2,1)S(1)} async-done(((bf16[8,1,2,3,1,24]{0,2,3,4,1,5:T(2,128)(2,1)}), bf16[8,1,2,3,1,24]{0,2,3,4,1,5:T(2,128)(2,1)S(1)}, u32[]{:S(2)}, u32[]{:S(2)}) %all-to-all-start.2) | async-done | bytes 2336 | tf_op jit(solution)/shard_map/all_to_all | solution.py:118
  79.2 3.3 %all-to-all-start.4 = ((bf16[8,1,2,3,1,24]{0,2,3,4,1,5:T(2,128)(2,1)}), bf16[8,1,2,3,1,24]{0,2,3,4,1,5:T(2,128)(2,1)S(1)}, u32[]{:S(2)}, u32[]{:S(2)}) async-start(bf16[8,1,2,3,1,24]{0,2,3,4,1,5:T(2,128)(2,1)} %copy.112), calls=%async_computation.4 | async-start | bytes 73728 | tf_op jit(solution)/shard_map/all_to_all | solution.py:118
  82.6 0.4 fusion.21
  83.0 0.7 copy.107
  83.7 5.5 %all-to-all-done.4 = bf16[8,1,2,3,1,24]{0,2,3,4,1,5:T(2,128)(2,1)S(1)} async-done(((bf16[8,1,2,3,1,24]{0,2,3,4,1,5:T(2,128)(2,1)}), bf16[8,1,2,3,1,24]{0,2,3,4,1,5:T(2,128)(2,1)S(1)}, u32[]{:S(2)}, u32[]{:S(2)}) %all-to-all-start.4) | async-done | bytes 2336 | tf_op jit(solution)/shard_map/all_to_all | solution.py:118
  89.2 3.3 %all-to-all-start.3 = ((bf16[8,1,2,24,1,3]{0,2,5,4,1,3:T(2,128)(2,1)}), bf16[8,1,2,24,1,3]{0,2,5,4,1,3:T(2,128)(2,1)S(1)}, u32[]{:S(2)}, u32[]{:S(2)}) async-start(bf16[8,1,2,24,1,3]{0,2,5,4,1,3:T(2,128)(2,1)} %copy.107), calls=%async_computation.3 | async-start | bytes 73728 | tf_op jit(solution)/shard_map/all_to_all | solution.py:121
  92.6 0.4 fusion.18
  93.0 0.7 copy.116
  93.7 5.5 %all-to-all-done.3 = bf16[8,1,2,24,1,3]{0,2,5,4,1,3:T(2,128)(2,1)S(1)} async-done(((bf16[8,1,2,24,1,3]{0,2,5,4,1,3:T(2,128)(2,1)}), bf16[8,1,2,24,1,3]{0,2,5,4,1,3:T(2,128)(2,1)S(1)}, u32[]{:S(2)}, u32[]{:S(2)}) %all-to-all-start.3) | async-done | bytes 2336 | tf_op jit(solution)/shard_map/all_to_all | solution.py:121
  99.2 3.3 %all-to-all-start.5 = ((bf16[8,1,2,24,1,3]{0,2,5,4,1,3:T(2,128)(2,1)}), bf16[8,1,2,24,1,3]{0,2,5,4,1,3:T(2,128)(2,1)S(1)}, u32[]{:S(2)}, u32[]{:S(2)}) async-start(bf16[8,1,2,24,1,3]{0,2,5,4,1,3:T(2,128)(2,1)} %copy.116), calls=%async_computation.5 | async-start | bytes 73728 | tf_op jit(solution)/shard_map/all_to_all | solution.py:121
  102.6 0.2 fusion.7
  102.8 0.2 fusion.15
  103.0 6.2 %all-to-all-done.5 = bf16[8,1,2,24,1,3]{0,2,5,4,1,3:T(2,128)(2,1)S(1)} async-done(((bf16[8,1,2,24,1,3]{0,2,5,4,1,3:T(2,128)(2,1)}), bf16[8,1,2,24,1,3]{0,2,5,4,1,3:T(2,128)(2,1)S(1)}, u32[]{:S(2)}, u32[]{:S(2)}) %all-to-all-start.5) | async-done | bytes 2336 | tf_op jit(solution)/shard_map/all_to_all | solution.py:121
  109.2 0.2 fusion.9
  109.4 0.2 fusion.17
  109.6 10.3 %all-reduce.6 = (bf16[8,1,2,3,24]{4,0,3,2,1:T(8,128)(2,1)S(1)}, bf16[8,1,2,3,24]{4,0,3,2,1:T(8,128)(2,1)S(1)}) all-reduce(bf16[8,1,2,3,24]{4,0,3,2,1:T(8,128)(2,1)S(1)} %fusion.17, bf16[8,1,2,3,24]{4,0,3,2,1:T(8,128)(2,1)S(1)} %fusion.15), channel_id=5, replica_groups=mesh['wave'=8,'lev'=4] {'lev'}, use_global_device_ids=true, to_apply=%region_4.6.clone | all-reduce | flops 2304 | bytes 9216
  119.9 0.2 convolution_convert_fusion.2
  120.2 10.4 %all-reduce.5 = bf16[8,2,2,3,24]{4,0,3,2,1:T(8,128)(2,1)S(1)} all-reduce(bf16[8,2,2,3,24]{4,0,3,2,1:T(8,128)(2,1)S(1)} %convolution_convert_fusion.2), channel_id=6, replica_groups=mesh['wave'=8,'lev'=4] {'lev'}, use_global_device_ids=true, to_apply=%region_5.7.clone | all-reduce | flops 2304 | bytes 9216
  130.6 0.6 copy.120
  (45 shorter events, 0.7 us)
Async XLA Ops:
  0.6 46.0 %copy-start = (f32[8,8]{1,0:T(8,128)S(1)}, f32[8,8]{1,0:T(8,128)}, u32[]{:S(2)}) copy-start(f32[8,8]{1,0:T(8,128)} %param.16) | copy-start | bytes 772
  0.6 0.8 copy-start.2
  7.7 0.7 copy-start.1
  9.6 6.4 %copy-start.4 = (s32[24]{0:T(128)S(1)}, s32[24]{0:T(128)}, u32[]{:S(2)}) copy-start(s32[24]{0:T(128)} %param.11) | copy-start | bytes 292
  9.6 13.0 %all-to-all-start = ((bf16[8,2,432]{2,1,0:T(2,128)(2,1)}), bf16[8,2,432]{2,1,0:T(2,128)(2,1)S(1)}, u32[]{:S(2)}, u32[]{:S(2)}) async-start(bf16[8,2,432]{2,1,0:T(2,128)(2,1)} %reshape.468), calls=%async_computation | async-start | bytes 32768 | tf_op jit(solution)/shard_map/all_to_all | solution.py:129
  18.4 0.7 copy-start.6
  19.2 0.7 copy-start.7
  22.8 0.9 copy-start.3
  25.6 9.9 %all-to-all-start.1 = ((bf16[8,2,432]{2,1,0:T(2,128)(2,1)}), bf16[8,2,432]{2,1,0:T(2,128)(2,1)S(1)}, u32[]{:S(2)}, u32[]{:S(2)}) async-start(bf16[8,2,432]{2,1,0:T(2,128)(2,1)} %reshape.470), calls=%async_computation.1 | async-start | bytes 32768 | tf_op jit(solution)/shard_map/all_to_all | solution.py:130
  29.0 0.7 copy-start.8
  58.8 3.1 %collective-permute-start = (f32[2,1,2,3,24]{4,0,3,2,1:T(2,128)S(1)}, f32[2,1,2,3,24]{4,0,3,2,1:T(2,128)S(1)}, u32[]{:S(2)}, u32[]{:S(2)}) collective-permute-start(f32[2,1,2,3,24]{4,0,3,2,1:T(2,128)S(1)} %get-tuple-element.14), channel_id=1, source_target_pairs={{0,1},{1,2},{2,3},{3,0},{4,5},{5,6},{6,7},{7,4},{8,9},{9,10},{10,1... | collective-permute-start | bytes 3464 | tf_op jit(solution)/shard_map/ppermute | solution.py:97
  58.8 3.6 %collective-permute-start.3 = (f32[2,1,2,3,24]{4,0,3,2,1:T(2,128)S(1)}, f32[2,1,2,3,24]{4,0,3,2,1:T(2,128)S(1)}, u32[]{:S(2)}, u32[]{:S(2)}) collective-permute-start(f32[2,1,2,3,24]{4,0,3,2,1:T(2,128)S(1)} %get-tuple-element.19), channel_id=1, source_target_pairs={{0,1},{1,2},{2,3},{3,0},{4,5},{5,6},{6,7},{7,4},{8,9},{9,10},{10,1... | collective-permute-start | bytes 3464 | tf_op jit(solution)/shard_map/ppermute | solution.py:97
  61.9 3.1 %collective-permute-start.1 = (f32[2,1,2,3,24]{4,0,3,2,1:T(2,128)S(1)}, f32[2,1,2,3,24]{4,0,3,2,1:T(2,128)S(1)}, u32[]{:S(2)}, u32[]{:S(2)}) collective-permute-start(f32[2,1,2,3,24]{4,0,3,2,1:T(2,128)S(1)} %collective-permute-done), channel_id=1, source_target_pairs={{0,1},{1,2},{2,3},{3,0},{4,5},{5,6},{6,7},{7,4},{8,9},{9,10},{10,1... | collective-permute-start | bytes 3464 | tf_op jit(solution)/shard_map/ppermute | solution.py:97
  62.5 4.5 %collective-permute-start.4 = (f32[2,1,2,3,24]{4,0,3,2,1:T(2,128)S(1)}, f32[2,1,2,3,24]{4,0,3,2,1:T(2,128)S(1)}, u32[]{:S(2)}, u32[]{:S(2)}) collective-permute-start(f32[2,1,2,3,24]{4,0,3,2,1:T(2,128)S(1)} %collective-permute-done.3), channel_id=1, source_target_pairs={{0,1},{1,2},{2,3},{3,0},{4,5},{5,6},{6,7},{7,4},{8,9},{9,10},{10,1... | collective-permute-start | bytes 3464 | tf_op jit(solution)/shard_map/ppermute | solution.py:97
  64.9 3.2 %collective-permute-start.2 = (f32[2,1,2,3,24]{4,0,3,2,1:T(2,128)S(1)}, f32[2,1,2,3,24]{4,0,3,2,1:T(2,128)S(1)}, u32[]{:S(2)}, u32[]{:S(2)}) collective-permute-start(f32[2,1,2,3,24]{4,0,3,2,1:T(2,128)S(1)} %collective-permute-done.1), channel_id=1, source_target_pairs={{0,1},{1,2},{2,3},{3,0},{4,5},{5,6},{6,7},{7,4},{8,9},{9,10},{10,1... | collective-permute-start | bytes 3464 | tf_op jit(solution)/shard_map/ppermute | solution.py:97
  66.4 1.8 %copy-start.5 = (f32[8,8]{1,0:T(8,128)S(1)}, f32[8,8]{1,0:T(8,128)}, u32[]{:S(2)}) copy-start(f32[8,8]{1,0:T(8,128)} %param.15) | copy-start | bytes 772
  67.0 5.6 %collective-permute-start.5 = (f32[2,1,2,3,24]{4,0,3,2,1:T(2,128)S(1)}, f32[2,1,2,3,24]{4,0,3,2,1:T(2,128)S(1)}, u32[]{:S(2)}, u32[]{:S(2)}) collective-permute-start(f32[2,1,2,3,24]{4,0,3,2,1:T(2,128)S(1)} %collective-permute-done.4), channel_id=1, source_target_pairs={{0,1},{1,2},{2,3},{3,0},{4,5},{5,6},{6,7},{7,4},{8,9},{9,10},{10,1... | collective-permute-start | bytes 3464 | tf_op jit(solution)/shard_map/ppermute | solution.py:97
  69.2 10.0 %all-to-all-start.2 = ((bf16[8,1,2,3,1,24]{0,2,3,4,1,5:T(2,128)(2,1)}), bf16[8,1,2,3,1,24]{0,2,3,4,1,5:T(2,128)(2,1)S(1)}, u32[]{:S(2)}, u32[]{:S(2)}) async-start(bf16[8,1,2,3,1,24]{0,2,3,4,1,5:T(2,128)(2,1)} %copy.103), calls=%async_computation.2 | async-start | bytes 73728 | tf_op jit(solution)/shard_map/all_to_all | solution.py:118
  79.2 10.0 %all-to-all-start.4 = ((bf16[8,1,2,3,1,24]{0,2,3,4,1,5:T(2,128)(2,1)}), bf16[8,1,2,3,1,24]{0,2,3,4,1,5:T(2,128)(2,1)S(1)}, u32[]{:S(2)}, u32[]{:S(2)}) async-start(bf16[8,1,2,3,1,24]{0,2,3,4,1,5:T(2,128)(2,1)} %copy.112), calls=%async_computation.4 | async-start | bytes 73728 | tf_op jit(solution)/shard_map/all_to_all | solution.py:118
  89.2 10.0 %all-to-all-start.3 = ((bf16[8,1,2,24,1,3]{0,2,5,4,1,3:T(2,128)(2,1)}), bf16[8,1,2,24,1,3]{0,2,5,4,1,3:T(2,128)(2,1)S(1)}, u32[]{:S(2)}, u32[]{:S(2)}) async-start(bf16[8,1,2,24,1,3]{0,2,5,4,1,3:T(2,128)(2,1)} %copy.107), calls=%async_computation.3 | async-start | bytes 73728 | tf_op jit(solution)/shard_map/all_to_all | solution.py:121
  99.2 10.0 %all-to-all-start.5 = ((bf16[8,1,2,24,1,3]{0,2,5,4,1,3:T(2,128)(2,1)}), bf16[8,1,2,24,1,3]{0,2,5,4,1,3:T(2,128)(2,1)S(1)}, u32[]{:S(2)}, u32[]{:S(2)}) async-start(bf16[8,1,2,24,1,3]{0,2,5,4,1,3:T(2,128)(2,1)} %copy.116), calls=%async_computation.5 | async-start | bytes 73728 | tf_op jit(solution)/shard_map/all_to_all | solution.py:121
